TPU v7x, 32 devices: a whole 2x2x4 slice. The times are simulated.
32 devices in a mesh: row: 8 (over z, y), col: 2 (over core), layer: 2 (over x).
Axes of the slice: x: 2, y: 2, z: 4, core: 2. Of those that a mesh axis runs over, the one named last changes fastest.
Arguments:
- matrix: float32 [1, 8, 256, 4, 2, 256], P(None, 'row', None, None, 'col'), may hold values from -8 to 113.137085, as said below
Outputs:
- factored: float32 [1, 8, 256, 4, 2, 256], P(None, 'row', None, 'layer', 'col')
Inputs may be any that keep to these rules, and one draw needn't show every extreme that they name: `matrix`: viewed as in the first step it is symmetric, its leading 2 * 256 x 2 * 256 block is positive definite, and its diagonal entries lie between 2.5 and 5 times the square root of 512.
All inputs are finite; a program needn't handle non-finite values.
Results may differ from a plain program's by a relative error of at most 0.000059.
Values sent between devices are 32-bit elements; how exact they have to be, the bound alone decides.
No kernel may reach another device: no remote copies, remote signals or barrier semaphores. Data moves between devices by JAX's collectives and lax.ppermute only.
A program may use at most 128 MiB of HBM per device.

v0:
```python
import jax
import jax.numpy as jnp
from jax import lax
from jax.sharding import PartitionSpec as P

HIGH = lax.Precision.HIGHEST


def from_root(shard, axis, root):
    mine = lax.axis_index(axis) == root
    return lax.psum(jnp.where(mine, shard, jnp.zeros_like(shard)), axis)


def factor_block(diag_block):
    lower_fac = jnp.linalg.cholesky(diag_block)
    identity = jnp.eye(diag_block.shape[0], dtype=jnp.float32)
    inverse = lax.linalg.triangular_solve(lower_fac, identity, left_side=True, lower=True)
    return (lower_fac, inverse)


def on_device(matrix):
    row_total = lax.axis_size("row")
    col_total = lax.axis_size("col")
    layer_total = lax.axis_size("layer")
    grid_row = lax.axis_index("row")
    grid_col = lax.axis_index("col")
    grid_layer = lax.axis_index("layer")
    row_blocks = matrix.shape[0]
    block_size = matrix.shape[2]
    col_blocks = matrix.shape[3]
    half = block_size // layer_total
    owned = col_blocks // layer_total
    rows = row_blocks * block_size
    tile = matrix.reshape(rows, col_blocks * block_size)
    row_ids = jnp.arange(rows) // block_size * row_total + grid_row
    column = tile[:, :block_size]
    pending = None
    total = None
    panels = []
    for section in range(2):
        diag_block = from_root(column, "row", section % row_total)
        lower_fac, inverse = factor_block(diag_block)
        solved = jnp.dot(column, inverse.T, precision=HIGH, preferred_element_type=jnp.float32)
        repeated = jnp.tile(lower_fac, (row_blocks, 1))
        complete = jnp.where(
            row_ids[:, None] > section,
            solved,
            jnp.where(row_ids[:, None] == section, repeated, 0.0),
        )
        panels.append(complete)
        share = lax.dynamic_slice_in_dim(complete, grid_layer * half, half, 1)
        share = from_root(share, "col", section % col_total)
        gathered = lax.all_gather(
            share.reshape(row_blocks, 1, block_size, half), "row", axis=1, tiled=True
        )
        grouped = gathered.reshape(col_blocks, col_total, block_size, half)
        picked = lax.dynamic_index_in_dim(grouped, grid_col, 1, keepdims=False).reshape(
            col_blocks * block_size, half
        )
        update = lax.dot_general(
            share,
            picked,
            (((1,), (1,)), ((), ())),
            precision=HIGH,
            preferred_element_type=jnp.float32,
        )
        if section == 0:
            head = lax.psum(update[:, :block_size], "layer")
            column = tile[:, :block_size] - head
            pending = update
        else:
            total = pending + update
    reduced = lax.psum_scatter(
        total.reshape(rows, col_blocks, block_size), "layer", scatter_dimension=1, tiled=True
    )
    own_part = (
        lax.dynamic_slice_in_dim(
            tile.reshape(rows, col_blocks, block_size), grid_layer * owned, owned, 1
        )
        - reduced
    )
    replacement = jnp.where(grid_col == 0, panels[0], panels[1])
    global_ids = (grid_layer * owned + jnp.arange(owned)) * col_total + grid_col
    result = jnp.where((global_ids < 2)[None, :, None], replacement[:, None, :], own_part)
    return result.reshape(row_blocks, 1, block_size, owned, 1, block_size)


def solution(mesh):
    in_specs = (P(None, "row", None, None, "col", None),)
    out_specs = P(None, "row", None, "layer", "col", None)
    return jax.shard_map(
        on_device, mesh=mesh, in_specs=in_specs, out_specs=out_specs, check_vma=False
    )
```

profile of v0, /device:TPU:0, one launch (start us, length us, event | category | flops | bytes accessed | tf_op | source)
XLA Modules:
  0.0 472.5 jit_solution(6674159370767984335)
XLA Ops:
  6.5 2.3 copy.16
  8.9 0.7 slice_select_fusion
  9.8 74.7 %all-reduce.7.cloned.1.call-done = f32[256,256]{0,1:T(8,128)} async-done(((f32[256,256]{0,1:T(8,128)}), f32[256,256]{0,1:T(8,128)}) %all-reduce.7.cloned.1.call-update) | async-done | bytes 262160 | tf_op jit(solution)/shard_map/psum | solution.py:11
  84.4 1.1 copy.17
  85.7 11.7 %cholesky.130 = f32[128,128]{1,0:T(8,128)S(1)} custom-call(f32[128,128]{1,0:T(8,128)S(1)} %cholesky.194), custom_call_target="Cholesky" | custom-call | tf_op jit(solution)/shard_map/jit(cholesky)/cholesky | solution.py:15
  97.4 9.8 %custom-call.13 = f32[1,128,128]{1,2,0:T(8,128)S(1)} custom-call(f32[1,128,128]{2,1,0:T(8,128)S(1)} %get-tuple-element.62), custom_call_target="InvertDiagBlocksLowerTriangular" | custom-call | tf_op jit(solution)/shard_map/jit(cholesky)/cholesky | solution.py:15
  107.2 0.2 fusion.26
  107.4 0.3 convolution_subtract_fusion.3
  107.7 11.7 %cholesky.147 = f32[128,128]{1,0:T(8,128)S(1)} custom-call(f32[128,128]{1,0:T(8,128)S(1)} %convolution_subtract_fusion.3), custom_call_target="Cholesky" | custom-call | tf_op jit(solution)/shard_map/jit(cholesky)/cholesky | solution.py:15
  119.8 0.7 compare_reduce_fusion.2
  122.0 4.8 %while.4 = (s32[]{:T(128)}, f32[256,256]{0,1:T(8,128)S(1)}, s32[2,2]{1,0:T(2,128)S(1)}, f32[2,128,128]{2,1,0:T(8,128)S(1)}, s32[]{:T(128)}) while((s32[]{:T(128)}, f32[256,256]{0,1:T(8,128)S(1)}, s32[2,2]{1,0:T(2,128)S(1)}, f32[2,128,128]{2,1,0:T(8,128)S(1)}, s32[]{:T(128)}) %tuple.46), condition=%wide.while_cond, body=%wide.while_body.sunk | while | flops 2 | bytes 393321 | solution.py:17
  122.5 0.6 fusion.51
  123.1 1.4 dynamic-slice.13
  124.7 0.6 fusion.51
  125.3 1.4 dynamic-slice.13
  126.8 19.7 %custom-call.14 = f32[2,128,128]{1,2,0:T(8,128)S(1)} custom-call(f32[2,128,128]{2,1,0:T(8,128)S(1)} %get-tuple-element.21), custom_call_target="InvertDiagBlocksLowerTriangular" | custom-call | tf_op jit(solution)/shard_map/triangular_solve/custom-call.0 | solution.py:17
  146.5 0.3 fusion.18
  146.8 0.3 convolution_subtract_fusion.1
  147.1 0.3 fusion.25
  147.4 0.4 fusion
  147.8 0.7 dynamic-slice_select_fusion.1
  148.6 17.2 %all-reduce.9.cloned.1.call-done = f32[256,128]{0,1:T(8,128)} async-done(((f32[256,128]{0,1:T(8,128)}), f32[256,128]{0,1:T(8,128)}) %all-reduce.9.cloned.1.call-update) | async-done | bytes 131088 | tf_op jit(solution)/shard_map/psum | solution.py:11
  165.9 42.6 %all-gather.5.cloned.1.call-done = f32[2048,128]{0,1:T(8,128)} async-done(((f32[256,128]{0,1:T(8,128)}), f32[2048,128]{0,1:T(8,128)}) %all-gather.5.cloned.1.call-update) | async-done | bytes 1048592 | tf_op jit(solution)/shard_map/all_gather | solution.py:53
  208.5 2.1 reshape.86
  210.6 1.6 dynamic-slice_reduce_fusion.1
  212.3 0.8 copy-done.4
  213.1 1.0 fusion.36
  214.2 0.8 copy.36
  215.1 22.4 %all-reduce.11.cloned.1.call-done = f32[256,256]{0,1:T(8,128)} async-done(((f32[256,256]{0,1:T(8,128)}), f32[256,256]{0,1:T(8,128)}) %all-reduce.11.cloned.1.call-update) | async-done | bytes 262160 | tf_op jit(solution)/shard_map/psum | solution.py:68
  237.5 1.7 broadcast_select_fusion
  239.2 0.2 all-reduce.15.cloned.1.call-start
  239.5 72.3 %all-reduce.13.cloned.1.call-done = f32[256,256]{0,1:T(8,128)} async-done(((f32[256,256]{0,1:T(8,128)}), f32[256,256]{0,1:T(8,128)}) %all-reduce.13.cloned.1.call-update) | async-done | bytes 262160 | tf_op jit(solution)/shard_map/psum | solution.py:11
  311.8 1.1 copy.23
  313.0 11.7 %cholesky.164 = f32[128,128]{1,0:T(8,128)S(1)} custom-call(f32[128,128]{1,0:T(8,128)S(1)} %cholesky.197), custom_call_target="Cholesky" | custom-call | tf_op jit(solution)/shard_map/jit(cholesky)/cholesky | solution.py:15
  324.8 9.8 %custom-call.15 = f32[1,128,128]{1,2,0:T(8,128)S(1)} custom-call(f32[1,128,128]{2,1,0:T(8,128)S(1)} %get-tuple-element.60), custom_call_target="InvertDiagBlocksLowerTriangular" | custom-call | tf_op jit(solution)/shard_map/jit(cholesky)/cholesky | solution.py:15
  334.6 0.2 fusion.22
  334.8 0.3 convolution_subtract_fusion.2
  335.1 11.7 %cholesky.181 = f32[128,128]{1,0:T(8,128)S(1)} custom-call(f32[128,128]{1,0:T(8,128)S(1)} %convolution_subtract_fusion.2), custom_call_target="Cholesky" | custom-call | tf_op jit(solution)/shard_map/jit(cholesky)/cholesky | solution.py:15
  347.1 0.7 compare_reduce_fusion
  347.8 0.6 compare_reduce_fusion.1
  349.8 4.4 while.5
  350.1 0.6 fusion.52
  350.7 1.4 dynamic-slice.15
  352.2 0.6 fusion.52
  352.8 1.4 dynamic-slice.15
  354.2 19.7 %custom-call.16 = f32[2,128,128]{1,2,0:T(8,128)S(1)} custom-call(f32[2,128,128]{2,1,0:T(8,128)S(1)} %get-tuple-element.22), custom_call_target="InvertDiagBlocksLowerTriangular" | custom-call | tf_op jit(solution)/shard_map/triangular_solve/custom-call.0 | solution.py:17
  373.9 0.3 fusion.16
  374.2 0.3 convolution_subtract_fusion
  374.6 0.3 fusion.21
  374.9 0.6 copy-done.3
  375.5 0.4 broadcast_select_fusion.1
  375.9 0.7 dynamic-slice_select_fusion
  376.7 17.2 %all-reduce.15.cloned.1.call-done = f32[256,128]{0,1:T(8,128)} async-done(((f32[256,128]{0,1:T(8,128)}), f32[256,128]{0,1:T(8,128)}) %all-reduce.15.cloned.1.call-update) | async-done | bytes 131088 | tf_op jit(solution)/shard_map/psum | solution.py:11
  393.9 42.6 %all-gather.7.cloned.1.call-done = f32[2048,128]{0,1:T(8,128)} async-done(((f32[256,128]{0,1:T(8,128)}), f32[2048,128]{0,1:T(8,128)}) %all-gather.7.cloned.1.call-update) | async-done | bytes 1048592 | tf_op jit(solution)/shard_map/all_gather | solution.py:53
  436.6 2.1 reshape.89
  438.7 1.6 dynamic-slice_reduce_fusion
  440.4 0.8 copy-done.5
  441.2 1.0 convolution_add_fusion
  442.2 1.1 copy.42
  443.4 1.2 copy-done
  444.5 0.4 constant_dynamic-slice_fusion.2
  445.0 17.9 %reduce-scatter.2.cloned.1.call-done = f32[256,2,256]{2,0,1:T(8,128)} async-done(((f32[256,4,256]{2,0,1:T(8,128)}), f32[256,2,256]{2,0,1:T(8,128)}) %reduce-scatter.2.cloned.1.call-update) | async-done | bytes 524304 | tf_op jit(solution)/shard_map/reduce_scatter | solution.py:73
  462.9 1.2 fusion.2
  464.1 1.3 copy.32
  (69 shorter events, 2.2 us)
Async XLA Ops:
  6.5 77.9 %all-reduce.7.cloned.1.call-start = ((), (), s32[]{:S(2)}) async-start(), calls=%async_computation.1 | async-start | bytes 524288 | tf_op jit(solution)/shard_map/psum | solution.py:11
  9.6 156.2 %all-reduce.9.cloned.1.call-start = ((), (), s32[]{:S(2)}) async-start(), calls=%async_computation.2 | async-start | bytes 262144 | tf_op jit(solution)/shard_map/psum | solution.py:11
  84.4 1.2 copy-start.1
  148.5 60.0 %all-gather.5.cloned.1.call-start = ((), (), s32[]{:S(2)}) async-start(), calls=%async_computation.7 | async-start | bytes 1179648 | tf_op jit(solution)/shard_map/all_gather | solution.py:53
  165.8 71.7 %all-reduce.11.cloned.1.call-start = ((), (), s32[]{:S(2)}) async-start(), calls=%async_computation.3 | async-start | bytes 524288 | tf_op jit(solution)/shard_map/psum | solution.py:68
  212.2 0.9 copy-start.4
  215.0 96.7 %all-reduce.13.cloned.1.call-start = ((), (), s32[]{:S(2)}) async-start(), calls=%async_computation.4 | async-start | bytes 524288 | tf_op jit(solution)/shard_map/psum | solution.py:11
  239.2 154.7 %all-reduce.15.cloned.1.call-start = ((), (), s32[]{:S(2)}) async-start(), calls=%async_computation.5 | async-start | bytes 262144 | tf_op jit(solution)/shard_map/psum | solution.py:11
  311.8 1.2 copy-start.2
  374.6 1.0 copy-start.3
  376.6 59.9 %all-gather.7.cloned.1.call-start = ((), (), s32[]{:S(2)}) async-start(), calls=%async_computation.8 | async-start | bytes 1179648 | tf_op jit(solution)/shard_map/all_gather | solution.py:53
  393.9 69.0 %reduce-scatter.2.cloned.1.call-start = ((), (), s32[]{:S(2)}) async-start(), calls=%async_computation.6 | async-start | bytes 1572864 | tf_op jit(solution)/shard_map/reduce_scatter | solution.py:73
  440.3 0.9 copy-start.5
  443.3 1.2 copy-start
Sparse Core Ops, SparseCore 0:
  10.7 73.7 all-reduce.6
  148.7 17.0 all-reduce.8
  167.8 40.5 all-gather.4
  215.2 22.2 all-reduce.10
  240.7 71.0 all-reduce.12
  376.7 17.0 all-reduce.14
  395.9 40.5 all-gather.6
  443.5 19.3 reduce-scatter.1
where the time goes:
time: 481 us; the launch traced here: 472 us
  waiting for transfers between devices  307 us (64%)
  other arithmetic  113 us (23%)
  local copies, waits for them, and re-layouts  28.5 us (6%)
  between operations  16.8 us (3%)
  matrix products  5.65 us (1%)
    psum x4, waiting for transfers between devices, from_root(): return lax.psum(jnp.where(mine, shard, jnp.zeros_like(shard)), axis)  181 us
    all_gather x2, waiting for transfers between devices, on_device(): lax.all_gather(share.reshape(row_blocks, 1, block_size, half), 'row', axi...  85.2 us
    another operation x13, other arithmetic, factor_block(): lower_fac = jnp.linalg.cholesky(diag_block)  68.7 us
    another operation x5, other arithmetic, factor_block(): lax.linalg.triangular_solve(lower_fac, identity, left_side=True, lower=True)  39.4 us
    psum x1, waiting for transfers between devices, on_device(): head = lax.psum(update[:, :block_size], 'layer')  22.4 us
    reduce_scatter x1, waiting for transfers between devices, on_device(): lax.psum_scatter(total.reshape(rows, col_blocks, block_size), 'layer', sc...  17.9 us
  transfers between devices with their start and end apart: 8, of which 8 were waited for; matrix products, arithmetic and copies ran while one was open for 0% of the time, Pallas kernels for 0%

commit v1 on v0

--- a/solution.py
+++ b/solution.py
@@ -2,6 +2,7 @@
 import jax.numpy as jnp
 from jax import lax
 from jax.sharding import PartitionSpec as P
+from jax.lax import axis_index, axis_size, ppermute
 
 HIGH = lax.Precision.HIGHEST
 
@@ -50,9 +51,35 @@
         panels.append(complete)
         share = lax.dynamic_slice_in_dim(complete, grid_layer * half, half, 1)
         share = from_root(share, "col", section % col_total)
-        gathered = lax.all_gather(
-            share.reshape(row_blocks, 1, block_size, half), "row", axis=1, tiled=True
-        )
+
+        def turn_the_heads(frame_in):
+            main, outcome_arr, clean = (axis_size("row"), axis_index("row"), frame_in.shape[1])
+            all_blocks = [k0 * main if ii == 1 else k0 for ii, k0 in enumerate(frame_in.shape)]
+            z_new = lax.dynamic_update_slice_in_dim(
+                jnp.zeros(all_blocks, frame_in.dtype), frame_in, outcome_arr * clean, axis=1
+            )
+            w_next = k_now = frame_in
+            for h in range(1, main // 2 + 1):
+                w_next = ppermute(
+                    w_next,
+                    axis_name="row",
+                    perm=list(map(lambda ii: (ii, (ii + 1) % main), range(main))),
+                )
+                z_new = lax.dynamic_update_slice_in_dim(
+                    z_new, w_next, (outcome_arr - h) % main * clean, axis=1
+                )
+                if 2 * h < main:
+                    k_now = ppermute(
+                        k_now,
+                        axis_name="row",
+                        perm=list(map(lambda ii: (ii, (ii - 1) % main), range(main))),
+                    )
+                    z_new = lax.dynamic_update_slice_in_dim(
+                        z_new, k_now, (outcome_arr + h) % main * clean, axis=1
+                    )
+            return z_new
+
+        gathered = turn_the_heads(share.reshape(row_blocks, 1, block_size, half))
         grouped = gathered.reshape(col_blocks, col_total, block_size, half)
         picked = lax.dynamic_index_in_dim(grouped, grid_col, 1, keepdims=False).reshape(
             col_blocks * block_size, half

time: 481 us -> 441 us (0.917); the launches traced: 472 us -> 441 us
  waiting for transfers between devices: 307 us -> 255 us
  starting transfers between devices: 0.46 us -> 27.9 us
  local copies, waits for them, and re-layouts: 28.5 us -> 22.1 us
    all_gather x2 -> x0, waiting for transfers between devices: 85.2 us -> none  [on_device(): lax.all_gather(share.reshape(row_blocks, 1, block_size, half), 'row', axi...]
    ppermute x0 -> x14, waiting for transfers between devices: none -> 34.4 us  [the longest x8 29.5 us: turn_the_heads(): ppermute(w_next, axis_name='row', perm=list(map(lambda ii: (ii, (ii + 1)...]
    ppermute x0 -> x14, starting transfers between devices: none -> 27.6 us  [the longest x6 20.1 us: turn_the_heads(): ppermute(k_now, axis_name='row', perm=list(map(lambda ii: (ii, (ii - 1) %...]
  transfers between devices with their start and end apart: 8 -> 20, of which waited for: 8 -> 17; matrix products, arithmetic and copies ran while one was open for 0% -> 1% of each run, Pallas kernels for 0% -> 0%
where the time goes in v1:
time: 441 us
  waiting for transfers between devices  255 us (58%)
  other arithmetic  113 us (26%)
  starting transfers between devices  27.9 us (6%)
  local copies, waits for them, and re-layouts  22.1 us (5%)
  between operations  16.8 us (4%)
  matrix products  5.65 us (1%)
    psum x4, waiting for transfers between devices, from_root(): return lax.psum(jnp.where(mine, shard, jnp.zeros_like(shard)), axis)  182 us
    another operation x13, other arithmetic, factor_block(): lower_fac = jnp.linalg.cholesky(diag_block)  68.6 us
    another operation x5, other arithmetic, factor_block(): lax.linalg.triangular_solve(lower_fac, identity, left_side=True, lower=True)  39.4 us
    ppermute x8, waiting for transfers between devices, turn_the_heads(): ppermute(w_next, axis_name='row', perm=list(map(lambda ii: (ii, (ii + 1)...  29.5 us
    psum x1, waiting for transfers between devices, on_device(): head = lax.psum(update[:, :block_size], 'layer')  22.3 us
    ppermute x6, starting transfers between devices, turn_the_heads(): ppermute(k_now, axis_name='row', perm=list(map(lambda ii: (ii, (ii - 1) %...  20.1 us
    reduce_scatter x1, waiting for transfers between devices, on_device(): lax.psum_scatter(total.reshape(rows, col_blocks, block_size), 'layer', sc...  16.2 us
  transfers between devices with their start and end apart: 20, of which 17 were waited for; matrix products, arithmetic and copies ran while one was open for 1% of the time, Pallas kernels for 0%

profile of v1, /device:TPU:0, one launch (start us, length us, event | category | flops | bytes accessed | tf_op | source)
XLA Modules:
  0.0 440.7 jit_solution(3799404772581854445)
XLA Ops:
  6.5 2.3 copy.60
  8.9 0.7 slice_select_fusion
  9.8 74.7 %all-reduce.7.cloned.1.call-done = f32[256,256]{0,1:T(8,128)} async-done(((f32[256,256]{0,1:T(8,128)}), f32[256,256]{0,1:T(8,128)}) %all-reduce.7.cloned.1.call-update) | async-done | bytes 262160 | tf_op jit(solution)/shard_map/psum | solution.py:12
  84.4 1.1 copy.61
  85.7 11.7 %cholesky.130 = f32[128,128]{1,0:T(8,128)S(1)} custom-call(f32[128,128]{1,0:T(8,128)S(1)} %cholesky.194), custom_call_target="Cholesky" | custom-call | tf_op jit(solution)/shard_map/jit(cholesky)/cholesky | solution.py:16
  97.4 9.8 %custom-call.13 = f32[1,128,128]{1,2,0:T(8,128)S(1)} custom-call(f32[1,128,128]{2,1,0:T(8,128)S(1)} %get-tuple-element.78), custom_call_target="InvertDiagBlocksLowerTriangular" | custom-call | tf_op jit(solution)/shard_map/jit(cholesky)/cholesky | solution.py:16
  107.7 11.7 %cholesky.147 = f32[128,128]{1,0:T(8,128)S(1)} custom-call(f32[128,128]{1,0:T(8,128)S(1)} %convolution_subtract_fusion.3), custom_call_target="Cholesky" | custom-call | tf_op jit(solution)/shard_map/jit(cholesky)/cholesky | solution.py:16
  119.8 0.7 compare_reduce_fusion.2
  122.0 4.5 %while.4 = (s32[]{:T(128)}, f32[256,256]{0,1:T(8,128)S(1)}, s32[2,2]{1,0:T(2,128)S(1)}, f32[2,128,128]{2,1,0:T(8,128)S(1)}, s32[]{:T(128)}) while((s32[]{:T(128)}, f32[256,256]{0,1:T(8,128)S(1)}, s32[2,2]{1,0:T(2,128)S(1)}, f32[2,128,128]{2,1,0:T(8,128)S(1)}, s32[]{:T(128)}) %tuple.50), condition=%wide.while_cond, body=%wide.while_body.sunk | while | flops 2 | bytes 393321 | solution.py:18
  122.2 0.6 fusion.51
  122.8 1.4 dynamic-slice.13
  124.4 0.6 fusion.51
  125.0 1.4 dynamic-slice.13
  126.5 19.7 %custom-call.14 = f32[2,128,128]{1,2,0:T(8,128)S(1)} custom-call(f32[2,128,128]{2,1,0:T(8,128)S(1)} %get-tuple-element.21), custom_call_target="InvertDiagBlocksLowerTriangular" | custom-call | tf_op jit(solution)/shard_map/triangular_solve/custom-call.0 | solution.py:18
  147.6 0.7 dynamic-slice_select_fusion.1
  148.3 17.2 %all-reduce.9.cloned.1.call-done = f32[256,128]{0,1:T(8,128)} async-done(((f32[256,128]{0,1:T(8,128)}), f32[256,128]{0,1:T(8,128)}) %all-reduce.9.cloned.1.call-update) | async-done | bytes 131088 | tf_op jit(solution)/shard_map/psum | solution.py:12
  165.5 1.8 collective-permute-start
  167.4 3.7 collective-permute-start.1
  171.2 3.2 collective-permute-done
  174.5 1.7 collective-permute-start.2
  176.2 3.5 collective-permute-start.3
  179.7 2.4 collective-permute-done.2
  182.3 1.5 collective-permute-start.4
  183.9 3.7 collective-permute-start.5
  187.5 2.5 collective-permute-done.4
  190.4 7.5 %collective-permute-done.6 = f32[1,1,256,128]{2,3,1,0:T(8,128)S(1)} collective-permute-done((f32[1,1,256,128]{2,3,1,0:T(8,128)S(1)}, f32[1,1,256,128]{2,3,1,0:T(8,128)S(1)}, u32[]{:S(2)}, u32[]{:S(2)}) %collective-permute-start.6) | collective-permute-done | bytes 131104 | tf_op jit(solution)/shard_map/ppermute | solution.py:63
  198.1 1.0 fusion.36
  199.1 0.8 copy.96
  200.1 22.3 %all-reduce.11.cloned.1.call-done = f32[256,256]{0,1:T(8,128)} async-done(((f32[256,256]{0,1:T(8,128)}), f32[256,256]{0,1:T(8,128)}) %all-reduce.11.cloned.1.call-update) | async-done | bytes 262160 | tf_op jit(solution)/shard_map/psum | solution.py:95
  222.4 1.7 broadcast_select_fusion
  224.2 72.5 %all-reduce.13.cloned.1.call-done = f32[256,256]{0,1:T(8,128)} async-done(((f32[256,256]{0,1:T(8,128)}), f32[256,256]{0,1:T(8,128)}) %all-reduce.13.cloned.1.call-update) | async-done | bytes 262160 | tf_op jit(solution)/shard_map/psum | solution.py:12
  296.7 1.1 copy.75
  297.9 11.7 %cholesky.164 = f32[128,128]{1,0:T(8,128)S(1)} custom-call(f32[128,128]{1,0:T(8,128)S(1)} %cholesky.197), custom_call_target="Cholesky" | custom-call | tf_op jit(solution)/shard_map/jit(cholesky)/cholesky | solution.py:16
  309.7 9.8 %custom-call.15 = f32[1,128,128]{1,2,0:T(8,128)S(1)} custom-call(f32[1,128,128]{2,1,0:T(8,128)S(1)} %get-tuple-element.76), custom_call_target="InvertDiagBlocksLowerTriangular" | custom-call | tf_op jit(solution)/shard_map/jit(cholesky)/cholesky | solution.py:16
  320.0 11.7 %cholesky.181 = f32[128,128]{1,0:T(8,128)S(1)} custom-call(f32[128,128]{1,0:T(8,128)S(1)} %convolution_subtract_fusion.2), custom_call_target="Cholesky" | custom-call | tf_op jit(solution)/shard_map/jit(cholesky)/cholesky | solution.py:16
  332.0 0.7 compare_reduce_fusion
  332.7 0.6 compare_reduce_fusion.1
  334.7 4.4 %while.5 = (s32[]{:T(128)}, f32[256,256]{0,1:T(8,128)S(1)}, s32[2,2]{1,0:T(2,128)S(1)}, f32[2,128,128]{2,1,0:T(8,128)S(1)}, s32[]{:T(128)}) while((s32[]{:T(128)}, f32[256,256]{0,1:T(8,128)S(1)}, s32[2,2]{1,0:T(2,128)S(1)}, f32[2,128,128]{2,1,0:T(8,128)S(1)}, s32[]{:T(128)}) %tuple.68), condition=%wide.while_cond.clone, body=%wide.while_body.clone.sunk | while | flops 2 | bytes 393321 | solution.py:18
  335.0 0.6 fusion.52
  335.5 1.4 dynamic-slice.15
  337.1 0.6 fusion.52
  337.6 1.4 dynamic-slice.15
  339.1 19.7 %custom-call.16 = f32[2,128,128]{1,2,0:T(8,128)S(1)} custom-call(f32[2,128,128]{2,1,0:T(8,128)S(1)} %get-tuple-element.22), custom_call_target="InvertDiagBlocksLowerTriangular" | custom-call | tf_op jit(solution)/shard_map/triangular_solve/custom-call.0 | solution.py:18
  359.8 0.6 copy-done.3
  360.8 0.7 dynamic-slice_select_fusion
  361.6 17.2 %all-reduce.15.cloned.1.call-done = f32[256,128]{0,1:T(8,128)} async-done(((f32[256,128]{0,1:T(8,128)}), f32[256,128]{0,1:T(8,128)}) %all-reduce.15.cloned.1.call-update) | async-done | bytes 131088 | tf_op jit(solution)/shard_map/psum | solution.py:12
  378.8 1.8 collective-permute-start.7
  380.6 1.0 copy.83
  381.6 3.0 collective-permute-start.8
  384.7 2.9 collective-permute-done.7
  387.8 2.0 collective-permute-done.8
  389.9 3.2 collective-permute-start.10
  393.1 2.3 collective-permute-done.9
  395.9 1.8 collective-permute-done.10
  397.8 3.1 collective-permute-start.12
  400.9 2.4 collective-permute-done.11
  403.9 1.0 collective-permute-done.12
  405.0 6.1 %collective-permute-done.13 = f32[1,1,256,128]{2,3,1,0:T(8,128)S(1)} collective-permute-done((f32[1,1,256,128]{2,3,1,0:T(8,128)S(1)}, f32[1,1,256,128]{2,3,1,0:T(8,128)S(1)}, u32[]{:S(2)}, u32[]{:S(2)}) %collective-permute-start.13) | collective-permute-done | bytes 131104 | tf_op jit(solution)/shard_map/ppermute | solution.py:63
  411.3 1.0 convolution_add_fusion
  412.4 1.1 copy.100
  413.5 1.2 copy-done
  415.2 16.2 %reduce-scatter.2.cloned.1.call-done = f32[256,2,256]{2,0,1:T(8,128)} async-done(((f32[256,4,256]{2,0,1:T(8,128)}), f32[256,2,256]{2,0,1:T(8,128)}) %reduce-scatter.2.cloned.1.call-update) | async-done | bytes 524304 | tf_op jit(solution)/shard_map/reduce_scatter | solution.py:100
  431.4 1.2 fusion.2
  432.5 1.3 copy.92
  (121 shorter events, 8.5 us)
Async XLA Ops:
  6.5 77.9 %all-reduce.7.cloned.1.call-start = ((), (), s32[]{:S(2)}) async-start(), calls=%async_computation.1 | async-start | bytes 524288 | tf_op jit(solution)/shard_map/psum | solution.py:12
  9.6 155.9 %all-reduce.9.cloned.1.call-start = ((), (), s32[]{:S(2)}) async-start(), calls=%async_computation.2 | async-start | bytes 262144 | tf_op jit(solution)/shard_map/psum | solution.py:12
  84.4 1.2 copy-start.1
  148.3 74.1 %all-reduce.11.cloned.1.call-start = ((), (), s32[]{:S(2)}) async-start(), calls=%async_computation.3 | async-start | bytes 524288 | tf_op jit(solution)/shard_map/psum | solution.py:95
  165.5 1.8 copy-start.4
  165.5 8.8 %collective-permute-start = (f32[1,1,256,128]{2,3,1,0:T(8,128)}, f32[1,1,256,128]{2,3,1,0:T(8,128)S(1)}, u32[]{:S(2)}, u32[]{:S(2)}) collective-permute-start(f32[1,1,256,128]{2,3,1,0:T(8,128)} %bitcast.95), channel_id=1, source_target_pairs={{0,4},{4,8},{8,12},{12,16},{16,20},{20,24},{24,28},{28,0},{1,5},{5... | collective-permute-start | bytes 393224 | tf_op jit(solution)/shard_map/ppermute | solution.py:63
  167.4 8.7 %collective-permute-start.1 = (f32[1,1,256,128]{2,3,1,0:T(8,128)S(1)}, f32[1,1,256,128]{2,3,1,0:T(8,128)S(1)}, u32[]{:S(2)}, u32[]{:S(2)}) collective-permute-start(f32[1,1,256,128]{2,3,1,0:T(8,128)S(1)} %bitcast.97), channel_id=1, source_target_pairs={{0,28},{4,0},{8,4},{12,8},{16,12},{20,16},{24,20},{28,24},{1,29},{... | collective-permute-start | bytes 393224 | tf_op jit(solution)/shard_map/ppermute | solution.py:72
  174.5 7.7 %collective-permute-start.2 = (f32[1,1,256,128]{2,3,1,0:T(8,128)S(1)}, f32[1,1,256,128]{2,3,1,0:T(8,128)S(1)}, u32[]{:S(2)}, u32[]{:S(2)}) collective-permute-start(f32[1,1,256,128]{2,3,1,0:T(8,128)S(1)} %collective-permute-done), channel_id=1, source_target_pairs={{0,4},{4,8},{8,12},{12,16},{16,20},{20,24},{24,28},{28,0},{1,5},{5... | collective-permute-start | bytes 393224 | tf_op jit(solution)/shard_map/ppermute | solution.py:63
  176.2 7.5 %collective-permute-start.3 = (f32[1,1,256,128]{2,3,1,0:T(8,128)S(1)}, f32[1,1,256,128]{2,3,1,0:T(8,128)S(1)}, u32[]{:S(2)}, u32[]{:S(2)}) collective-permute-start(f32[1,1,256,128]{2,3,1,0:T(8,128)S(1)} %collective-permute-done.1), channel_id=1, source_target_pairs={{0,28},{4,0},{8,4},{12,8},{16,12},{20,16},{24,20},{28,24},{1,29},{... | collective-permute-start | bytes 393224 | tf_op jit(solution)/shard_map/ppermute | solution.py:72
  182.3 7.8 %collective-permute-start.4 = (f32[1,1,256,128]{2,3,1,0:T(8,128)S(1)}, f32[1,1,256,128]{2,3,1,0:T(8,128)S(1)}, u32[]{:S(2)}, u32[]{:S(2)}) collective-permute-start(f32[1,1,256,128]{2,3,1,0:T(8,128)S(1)} %collective-permute-done.2), channel_id=1, source_target_pairs={{0,4},{4,8},{8,12},{12,16},{16,20},{20,24},{24,28},{28,0},{1,5},{5... | collective-permute-start | bytes 393224 | tf_op jit(solution)/shard_map/ppermute | solution.py:63
  183.9 6.4 %collective-permute-start.5 = (f32[1,1,256,128]{2,3,1,0:T(8,128)S(1)}, f32[1,1,256,128]{2,3,1,0:T(8,128)S(1)}, u32[]{:S(2)}, u32[]{:S(2)}) collective-permute-start(f32[1,1,256,128]{2,3,1,0:T(8,128)S(1)} %collective-permute-done.3), channel_id=1, source_target_pairs={{0,28},{4,0},{8,4},{12,8},{16,12},{20,16},{24,20},{28,24},{1,29},{... | collective-permute-start | bytes 393224 | tf_op jit(solution)/shard_map/ppermute | solution.py:72
  190.2 7.7 %collective-permute-start.6 = (f32[1,1,256,128]{2,3,1,0:T(8,128)S(1)}, f32[1,1,256,128]{2,3,1,0:T(8,128)S(1)}, u32[]{:S(2)}, u32[]{:S(2)}) collective-permute-start(f32[1,1,256,128]{2,3,1,0:T(8,128)S(1)} %collective-permute-done.4), channel_id=1, source_target_pairs={{0,4},{4,8},{8,12},{12,16},{16,20},{20,24},{24,28},{28,0},{1,5},{5... | collective-permute-start | bytes 393224 | tf_op jit(solution)/shard_map/ppermute | solution.py:63
  200.0 96.7 %all-reduce.13.cloned.1.call-start = ((), (), s32[]{:S(2)}) async-start(), calls=%async_computation.4 | async-start | bytes 524288 | tf_op jit(solution)/shard_map/psum | solution.py:12
  224.1 154.7 %all-reduce.15.cloned.1.call-start = ((), (), s32[]{:S(2)}) async-start(), calls=%async_computation.5 | async-start | bytes 262144 | tf_op jit(solution)/shard_map/psum | solution.py:12
  296.7 1.2 copy-start.2
  359.5 1.0 copy-start.3
  361.5 69.9 %reduce-scatter.2.cloned.1.call-start = ((), (), s32[]{:S(2)}) async-start(), calls=%async_computation.6 | async-start | bytes 1572864 | tf_op jit(solution)/shard_map/reduce_scatter | solution.py:100
  378.8 2.8 copy-start.5
  378.8 8.8 %collective-permute-start.7 = (f32[1,1,256,128]{2,3,1,0:T(8,128)}, f32[1,1,256,128]{2,3,1,0:T(8,128)S(1)}, u32[]{:S(2)}, u32[]{:S(2)}) collective-permute-start(f32[1,1,256,128]{2,3,1,0:T(8,128)} %bitcast.98), channel_id=1, source_target_pairs={{0,4},{4,8},{8,12},{12,16},{16,20},{20,24},{24,28},{28,0},{1,5},{5... | collective-permute-start | bytes 393224 | tf_op jit(solution)/shard_map/ppermute | solution.py:63
  381.6 8.2 %collective-permute-start.8 = (f32[1,1,256,128]{2,3,1,0:T(8,128)S(1)}, f32[1,1,256,128]{2,3,1,0:T(8,128)S(1)}, u32[]{:S(2)}, u32[]{:S(2)}) collective-permute-start(f32[1,1,256,128]{2,3,1,0:T(8,128)S(1)} %bitcast.100), channel_id=1, source_target_pairs={{0,28},{4,0},{8,4},{12,8},{16,12},{20,16},{24,20},{28,24},{1,29},{... | collective-permute-start | bytes 393224 | tf_op jit(solution)/shard_map/ppermute | solution.py:72
  387.7 7.7 %collective-permute-start.9 = (f32[1,1,256,128]{2,3,1,0:T(8,128)S(1)}, f32[1,1,256,128]{2,3,1,0:T(8,128)S(1)}, u32[]{:S(2)}, u32[]{:S(2)}) collective-permute-start(f32[1,1,256,128]{2,3,1,0:T(8,128)S(1)} %collective-permute-done.7), channel_id=1, source_target_pairs={{0,4},{4,8},{8,12},{12,16},{16,20},{20,24},{24,28},{28,0},{1,5},{5... | collective-permute-start | bytes 393224 | tf_op jit(solution)/shard_map/ppermute | solution.py:63
  389.9 7.8 %collective-permute-start.10 = (f32[1,1,256,128]{2,3,1,0:T(8,128)S(1)}, f32[1,1,256,128]{2,3,1,0:T(8,128)S(1)}, u32[]{:S(2)}, u32[]{:S(2)}) collective-permute-start(f32[1,1,256,128]{2,3,1,0:T(8,128)S(1)} %collective-permute-done.8), channel_id=1, source_target_pairs={{0,28},{4,0},{8,4},{12,8},{16,12},{20,16},{24,20},{28,24},{1,29},{... | collective-permute-start | bytes 393224 | tf_op jit(solution)/shard_map/ppermute | solution.py:72
  395.5 7.8 %collective-permute-start.11 = (f32[1,1,256,128]{2,3,1,0:T(8,128)S(1)}, f32[1,1,256,128]{2,3,1,0:T(8,128)S(1)}, u32[]{:S(2)}, u32[]{:S(2)}) collective-permute-start(f32[1,1,256,128]{2,3,1,0:T(8,128)S(1)} %collective-permute-done.9), channel_id=1, source_target_pairs={{0,4},{4,8},{8,12},{12,16},{16,20},{20,24},{24,28},{28,0},{1,5},{5... | collective-permute-start | bytes 393224 | tf_op jit(solution)/shard_map/ppermute | solution.py:63
  397.8 7.1 %collective-permute-start.12 = (f32[1,1,256,128]{2,3,1,0:T(8,128)S(1)}, f32[1,1,256,128]{2,3,1,0:T(8,128)S(1)}, u32[]{:S(2)}, u32[]{:S(2)}) collective-permute-start(f32[1,1,256,128]{2,3,1,0:T(8,128)S(1)} %collective-permute-done.10), channel_id=1, source_target_pairs={{0,28},{4,0},{8,4},{12,8},{16,12},{20,16},{24,20},{28,24},{1,29},{... | collective-permute-start | bytes 393224 | tf_op jit(solution)/shard_map/ppermute | solution.py:72
  403.4 7.7 %collective-permute-start.13 = (f32[1,1,256,128]{2,3,1,0:T(8,128)S(1)}, f32[1,1,256,128]{2,3,1,0:T(8,128)S(1)}, u32[]{:S(2)}, u32[]{:S(2)}) collective-permute-start(f32[1,1,256,128]{2,3,1,0:T(8,128)S(1)} %collective-permute-done.11), channel_id=1, source_target_pairs={{0,4},{4,8},{8,12},{12,16},{16,20},{20,24},{24,28},{28,0},{1,5},{5... | collective-permute-start | bytes 393224 | tf_op jit(solution)/shard_map/ppermute | solution.py:63
  413.4 1.2 copy-start
Sparse Core Ops, SparseCore 0:
  10.7 73.7 all-reduce.6
  148.4 17.0 all-reduce.8
  200.1 22.2 all-reduce.10
  225.6 71.0 all-reduce.12
  361.6 17.0 all-reduce.14
  413.6 17.7 reduce-scatter.1
